TPU v7x, 256 devices: a whole 4x4x8 slice. The times are simulated.
256 devices in a mesh: group: 32 (over x, y, core), tp: 8 (over z).
Axes of the slice: x: 4, y: 4, z: 8, core: 2. Of those that a mesh axis runs over, the one named last changes fastest.
Arguments:
- hidden_in: bfloat16 [64, 3072], P('group'), may hold values from -6 to 6
- w_qkv: bfloat16 [3072, 2048], P(None, 'tp'), may hold values from -0.109375 to 0.109375
- w_out: bfloat16 [1536, 3072], P('tp'), may hold values from -0.15625 to 0.15625
- kv_pool: bfloat16 [2048, 128, 512], P(('group', 'tp'))
- page_table: int32 [64, 32], replicated, may hold values from 0 to 2047, as said below
- lengths: int32 [64], replicated, may hold values from 1 to 4096, as said below
Outputs:
- attn_proj: bfloat16 [64, 3072], P('group', 'tp')
Inputs may be any that keep to these rules, and one draw needn't show every extreme that they name: `page_table`: every pool slot is named by exactly one request page. `lengths`: some request has the full 32 * 128 cached tokens.
All inputs are finite; a program needn't handle non-finite values.
Results may differ from a plain program's by a relative error of at most 0.0085.
The roundings to bfloat16 on the way count: a program that leaves them out, or rounds other values in their place, can miss the bound.
Values may be sent and summed in bfloat16 or wider, within the bound.
A program may use at most 64 MiB of HBM per device.

v0:
```python
import jax
import jax.numpy as jnp
from jax import lax
from jax.sharding import PartitionSpec as P

HEADS = 12
KV_HEADS = 2
HEAD_DIM = 128


def on_device(hidden_in, w_qkv, w_out, kv_pool, page_table, lengths):
    qdim = HEADS * HEAD_DIM
    kdim = KV_HEADS * HEAD_DIM
    per_kv = HEADS // KV_HEADS
    scale = HEAD_DIM ** (-0.5)
    req_grp = hidden_in.shape[0]
    col_count = w_out.shape[0]
    col_start = lax.axis_index("tp") * col_count
    columns = jnp.dot(hidden_in, w_qkv, preferred_element_type=jnp.float32).astype(jnp.bfloat16)
    qkv = lax.all_gather(columns, "tp", axis=1, tiled=True)
    queries = lax.all_gather(qkv[:, :qdim], "group", axis=0, tiled=True)
    requests = queries.shape[0]
    slot_count = kv_pool.shape[0]
    page_len = kv_pool.shape[1]
    max_pages = page_table.shape[1]
    slot_ids = lax.axis_index(("group", "tp")) * slot_count + jnp.arange(
        slot_count, dtype=jnp.int32
    )
    match = page_table[:, :, None] == slot_ids[None, None, :]
    slot_req = jnp.sum(
        jnp.where(match, jnp.arange(requests, dtype=jnp.int32)[:, None, None], 0), axis=(0, 1)
    )
    slot_page = jnp.sum(
        jnp.where(match, jnp.arange(max_pages, dtype=jnp.int32)[None, :, None], 0), axis=(0, 1)
    )
    chosen = queries[slot_req].reshape(slot_count, KV_HEADS, per_kv, HEAD_DIM)
    keys = kv_pool[..., :kdim].reshape(slot_count, page_len, KV_HEADS, HEAD_DIM)
    values = kv_pool[..., kdim:].reshape(slot_count, page_len, KV_HEADS, HEAD_DIM)
    scores = jnp.einsum("pgjd,ptgd->pgjt", chosen, keys, preferred_element_type=jnp.float32) * scale
    position = slot_page[:, None] * page_len + jnp.arange(page_len, dtype=jnp.int32)[None, :]
    live = (position < lengths[slot_req][:, None])[:, None, None, :]
    top = jnp.max(jnp.where(live, scores, -1e30), axis=-1)
    probs = jnp.where(live, jnp.exp(scores - top[..., None]), 0.0).astype(jnp.bfloat16)
    total = jnp.sum(probs.astype(jnp.float32), axis=-1)
    weighted = jnp.einsum("pgjt,ptgd->pgjd", probs, values, preferred_element_type=jnp.float32)
    owner = slot_req[None, :] == jnp.arange(requests, dtype=jnp.int32)[:, None]
    req_top = jnp.max(jnp.where(owner[:, :, None, None], top[None], -1e30), axis=1)
    factor = jnp.exp(top - req_top[slot_req])
    onehot = owner.astype(jnp.float32)
    req_total = jnp.einsum(
        "rp,pgj->rgj", onehot, total * factor, precision=lax.Precision.HIGHEST
    ).reshape(requests, HEADS)
    req_sums = jnp.einsum(
        "rp,pgjd->rgjd", onehot, weighted * factor[..., None], precision=lax.Precision.HIGHEST
    ).reshape(requests, qdim)
    req_top = req_top.reshape(requests, HEADS)
    start = lax.axis_index("group") * req_grp
    peak_all = lax.pmax(req_top, ("group", "tp"))
    rescale = jnp.exp(req_top - peak_all)
    total_all, sums_all = lax.psum(
        (req_total * rescale, req_sums * jnp.repeat(rescale, HEAD_DIM, axis=1)), ("group", "tp")
    )
    peak = lax.dynamic_slice_in_dim(peak_all, start, req_grp, 0)
    whole = lax.dynamic_slice_in_dim(total_all, start, req_grp, 0)
    sums = lax.dynamic_slice_in_dim(sums_all, start, req_grp, 0)
    sums_part = lax.dynamic_slice_in_dim(sums, col_start, col_count, 1)
    own_q = qkv[:, :qdim].reshape(req_grp, KV_HEADS, per_kv, HEAD_DIM)
    own_k = qkv[:, qdim : qdim + kdim].reshape(req_grp, KV_HEADS, HEAD_DIM)
    own_v = qkv[:, qdim + kdim :].reshape(req_grp, KV_HEADS, HEAD_DIM)
    own_score = (
        jnp.einsum("rgjd,rgd->rgj", own_q, own_k, preferred_element_type=jnp.float32) * scale
    ).reshape(req_grp, HEADS)
    own_sums = jnp.broadcast_to(
        own_v.astype(jnp.float32)[:, :, None, :], (req_grp, KV_HEADS, per_kv, HEAD_DIM)
    ).reshape(req_grp, qdim)
    new_peak = jnp.maximum(peak, own_score)
    old_factor = jnp.exp(peak - new_peak)
    own_factor = jnp.exp(own_score - new_peak)
    new_whole = whole * old_factor + own_factor

    def pick(values_full):
        return lax.dynamic_slice_in_dim(values_full, col_start, col_count, 1)

    new_sums = sums_part * pick(jnp.repeat(old_factor, HEAD_DIM, axis=1)) + pick(
        own_sums * jnp.repeat(own_factor, HEAD_DIM, axis=1)
    )
    attn_part = (new_sums / pick(jnp.repeat(new_whole, HEAD_DIM, axis=1))).astype(jnp.bfloat16)
    partial_value = jnp.dot(attn_part, w_out, preferred_element_type=jnp.float32)
    return lax.psum_scatter(partial_value, "tp", scatter_dimension=1, tiled=True).astype(
        jnp.bfloat16
    )


def solution(mesh):
    in_specs = (
        P("group", None),
        P(None, "tp"),
        P("tp", None),
        P(("group", "tp"), None, None),
        P(),
        P(),
    )
    out_specs = P("group", "tp")
    return jax.shard_map(
        on_device, mesh=mesh, in_specs=in_specs, out_specs=out_specs, check_vma=False
    )
```

profile of v0, /device:TPU:2, one launch (start us, length us, event | category | flops | bytes accessed | tf_op | source)
XLA Modules:
  0.0 429.0 jit_solution(9588263399593622062)
XLA Ops:
  6.5 0.0 copy-start
  6.5 0.0 copy-start.1
  6.5 0.0 all-reduce.2.cloned.1.call-start
  6.5 1.1 fusion.1
  7.6 0.1 iota_compare_fusion
  7.7 0.2 copy-done
  8.0 1.0 convolution_convert_fusion
  9.0 19.1 %all_gather.6 = bf16[2,2048]{1,0:T(2,128)(2,1)S(1)} all-gather(bf16[2,256]{1,0:T(2,128)(2,1)S(1)} %convolution_convert_fusion), channel_id=1, replica_groups=mesh['group'=32,'tp'=8] {'tp'}, dimensions={1}, use_global_device_ids=true | all-gather | bytes 9216 | tf_op jit(solution)/shard_map/all_gather | solution.py:20
  28.1 24.7 %all-gather = bf16[32,2,1536]{2,1,0:T(2,128)(2,1)S(1)} all-gather(bf16[1,2,1536]{2,1,0:T(2,128)(2,1)S(1)} %get-tuple-element.19), channel_id=1, replica_groups=mesh['group'=32,'tp'=8] {'group'}, dimensions={0}, use_global_device_ids=true | all-gather | bytes 202752 | tf_op jit(solution)/shard_map/all_gather | solution.py:21
  52.8 0.1 reshape.166
  52.9 0.0 copy-done.1
  52.9 0.6 gather_fusion
  53.5 0.6 gather_fusion.1
  54.1 1.3 fusion.25
  55.4 0.3 copy.96
  55.7 0.1 add_compare_fusion
  55.8 0.3 select_reduce_fusion
  56.1 0.1 copy.81
  56.2 0.1 select_reduce_fusion.1
  56.3 0.1 copy.82
  56.4 0.3 copy.97
  56.7 0.2 convert_reduce_fusion
  56.9 0.1 copy.86
  57.0 74.0 %pmax.7 = f32[64,12]{1,0:T(8,128)S(1)} all-reduce(f32[64,12]{1,0:T(8,128)S(1)} %copy.86), channel_id=1, replica_groups=mesh['group'=32,'tp'=8] {'group','tp'}, use_global_device_ids=true, to_apply=%region_4.5 | all-reduce | flops 768 | bytes 6144 | tf_op jit(solution)/shard_map/pmax | solution.py:58
  131.0 0.6 gather_fusion.2
  131.6 0.2 fusion.5
  131.8 0.1 copy.88
  131.9 0.4 convolution_multiply_fusion
  132.3 0.4 fusion.2
  132.8 0.2 copy.84
  133.0 0.1 reshape.129
  133.1 0.0 copy-start.2
  133.2 0.2 broadcast_in_dim.104
  133.4 0.9 bitcast_multiply_fusion
  134.3 0.0 all-reduce.2.cloned.1.call-update
  134.3 0.0 reduce-scatter.4.cloned.1.call-start
  134.4 0.1 fusion.27
  134.5 0.1 reshape.134
  134.6 74.9 %psum.15 = f32[64,12]{1,0:T(8,128)S(1)} all-reduce(f32[64,12]{1,0:T(8,128)S(1)} %get-tuple-element.10), channel_id=1, replica_groups=mesh['group'=32,'tp'=8] {'group','tp'}, use_global_device_ids=true, to_apply=%region_7.8 | all-reduce | flops 768 | bytes 6144 | tf_op jit(solution)/shard_map/psum | solution.py:60
  209.5 0.1 broadcast_bitcast_fusion.2
  209.6 0.1 broadcast_bitcast_fusion
  209.7 168.6 %all-reduce.2.cloned.1.call-done = f32[64,1536]{1,0:T(8,128)} async-done(((f32[64,1536]{1,0:T(8,128)}), f32[64,1536]{1,0:T(8,128)}) %all-reduce.2.cloned.1.call-update) | async-done | bytes 393232 | tf_op jit(solution)/shard_map/psum | solution.py:60
  378.3 0.0 copy-done.2
  378.3 2.7 convolution_bitcast_fusion
  381.0 0.0 reduce-scatter.4.cloned.1.call-update
  381.0 39.5 %reduce-scatter.4.cloned.1.call-done = f32[384,2]{1,0:T(8,128)} async-done(((f32[3072,2]{1,0:T(8,128)}), f32[384,2]{1,0:T(8,128)}) %reduce-scatter.4.cloned.1.call-update) | async-done | bytes 3088
  420.5 1.6 copy.95
  (20 shorter events, 0.2 us)
Async XLA Ops:
  6.5 1.4 copy-start
  6.5 46.4 %copy-start.1 = (s32[64]{0:T(128)S(1)}, s32[64]{0:T(128)}, u32[]{:S(2)}) copy-start(s32[64]{0:T(128)} %param.11) | copy-start | bytes 772
  6.5 371.7 %all-reduce.2.cloned.1.call-start = ((), (), s32[]{:S(2)}) async-start(), calls=%async_computation.1 | async-start | bytes 786432 | tf_op jit(solution)/shard_map/psum | solution.py:60
  133.1 245.2 %copy-start.2 = (bf16[192,3072]{1,0:T(8,128)(2,1)S(1)}, bf16[192,3072]{1,0:T(8,128)(2,1)}, u32[]{:S(2)}) copy-start(bf16[192,3072]{1,0:T(8,128)(2,1)} %param.8) | copy-start | bytes 3538948
  134.3 286.2 %reduce-scatter.4.cloned.1.call-start = ((), (), s32[]{:S(2)}) async-start(), calls=%async_computation.2 | async-start | bytes 1769472
Sparse Core Ops, SparseCore 0:
  134.4 243.8 all-reduce.1
  381.1 39.3 reduce-scatter.3
where the time goes:
time: 430 us; the launch traced here: 429 us
  waiting for transfers between devices  208 us (48%)
  blocking collectives  193 us (45%)
  between operations  13.6 us (3%)
  local copies, waits for them, and re-layouts  6.81 us (2%)
  matrix products  5.21 us (1%)
    psum x1, waiting for transfers between devices, on_device(): lax.psum((req_total * rescale, req_sums * jnp.repeat(rescale, HEAD_DIM, a...  169 us
    psum x1, blocking collectives, on_device(): lax.psum((req_total * rescale, req_sums * jnp.repeat(rescale, HEAD_DIM, a...  74.9 us
    pmax x1, blocking collectives, on_device(): peak_all = lax.pmax(req_top, ('group', 'tp'))  74 us
    unnamed x3, waiting for transfers between devices  39.6 us
    all_gather x1, blocking collectives, on_device(): queries = lax.all_gather(qkv[:, :qdim], 'group', axis=0, tiled=True)  24.7 us
    all_gather x1, blocking collectives, on_device(): qkv = lax.all_gather(columns, 'tp', axis=1, tiled=True)  19.1 us
  transfers between devices with their start and end apart: 2, of which 2 were waited for; matrix products, arithmetic and copies ran while one was open for 0% of the time, Pallas kernels for 0%

commit v1 on v0

--- a/solution.py
+++ b/solution.py
@@ -6,6 +6,12 @@
 HEADS = 12
 KV_HEADS = 2
 HEAD_DIM = 128
+
+
+def laid_out(blocks, dim):
+    blocks = jnp.moveaxis(blocks, 0, dim)
+    lengths = blocks.shape
+    return blocks.reshape(*lengths[:dim], lengths[dim] * lengths[dim + 1], *lengths[dim + 2 :])
 
 
 def on_device(hidden_in, w_qkv, w_out, kv_pool, page_table, lengths):
@@ -17,7 +23,19 @@
     col_count = w_out.shape[0]
     col_start = lax.axis_index("tp") * col_count
     columns = jnp.dot(hidden_in, w_qkv, preferred_element_type=jnp.float32).astype(jnp.bfloat16)
-    qkv = lax.all_gather(columns, "tp", axis=1, tiled=True)
+    count = lax.axis_size("tp")
+    pairs = [(i, (i + 1) % count) for i in range(count)]
+    back = [(b, a) for a, b in pairs]
+    lower, upper = ([], [])
+    for step in range(count - 1):
+        if step % 2 == 0:
+            lower.append(lax.ppermute(lower[-1] if lower else columns, "tp", pairs))
+        else:
+            upper.append(lax.ppermute(upper[-1] if upper else columns, "tp", back))
+    blocks = jnp.stack([*lower[::-1], columns, *upper])
+    shift = lax.axis_index("tp") - len(lower)
+    blocks = blocks[(jnp.arange(count) - shift) % count]
+    qkv = laid_out(blocks, 1)
     queries = lax.all_gather(qkv[:, :qdim], "group", axis=0, tiled=True)
     requests = queries.shape[0]
     slot_count = kv_pool.shape[0]

time: 430 us -> 510 us (1.19)
  waiting for transfers between devices: 208 us -> 293 us
  blocking collectives: 193 us -> 175 us
  starting transfers between devices: 0.04 us -> 12.5 us
    psum x1, waiting for transfers between devices: 169 us -> 244 us  [on_device(): lax.psum((req_total * rescale, req_sums * jnp.repeat(rescale, HEAD_DIM, a...]
    all_gather x1 -> x0, blocking collectives: 19.1 us -> none  [on_device(): qkv = lax.all_gather(columns, 'tp', axis=1, tiled=True)]
    ppermute x0 -> x7, starting transfers between devices: none -> 12.5 us  [the longest x3 12.5 us: on_device(): upper.append(lax.ppermute(upper[-1] if upper else columns, 'tp', back))]
    ppermute x0 -> x7, waiting for transfers between devices: none -> 9.88 us  [the longest x4 9.54 us: on_device(): lower.append(lax.ppermute(lower[-1] if lower else columns, 'tp', pairs))]
  transfers between devices with their start and end apart: 2 -> 9, of which waited for: 2 -> 7; matrix products, arithmetic and copies ran while one was open for 0% -> 1% of each run, Pallas kernels for 0% -> 0%
where the time goes in v1:
time: 510 us; the launch traced here: 509 us
  waiting for transfers between devices  293 us (57%)
  blocking collectives  175 us (34%)
  between operations  13.6 us (3%)
  starting transfers between devices  12.5 us (2%)
  local copies, waits for them, and re-layouts  8.62 us (2%)
  matrix products  5.19 us (1%)
    psum x1, waiting for transfers between devices, on_device(): lax.psum((req_total * rescale, req_sums * jnp.repeat(rescale, HEAD_DIM, a...  244 us
    pmax x1, blocking collectives, on_device(): peak_all = lax.pmax(req_top, ('group', 'tp'))  76.4 us
    psum x1, blocking collectives, on_device(): lax.psum((req_total * rescale, req_sums * jnp.repeat(rescale, HEAD_DIM, a...  73.5 us
    unnamed x3, waiting for transfers between devices  39.6 us
    all_gather x1, blocking collectives, on_device(): queries = lax.all_gather(qkv[:, :qdim], 'group', axis=0, tiled=True)  24.7 us
    ppermute x3, starting transfers between devices, on_device(): upper.append(lax.ppermute(upper[-1] if upper else columns, 'tp', back))  12.5 us
  transfers between devices with their start and end apart: 9, of which 7 were waited for; matrix products, arithmetic and copies ran while one was open for 1% of the time, Pallas kernels for 0%

profile of v1, /device:TPU:2, one launch (start us, length us, event | category | flops | bytes accessed | tf_op | source)
XLA Modules:
  0.0 509.3 jit_solution(17270678631975801813)
XLA Ops:
  6.5 1.4 copy-done
  7.9 1.0 convolution_convert_fusion
  9.0 5.9 %collective-permute-start.4 = (bf16[2,256]{1,0:T(2,128)(2,1)S(1)}, bf16[2,256]{1,0:T(2,128)(2,1)S(1)}, u32[]{:S(2)}, u32[]{:S(2)}) collective-permute-start(bf16[2,256]{1,0:T(2,128)(2,1)S(1)} %convolution_convert_fusion), channel_id=1, source_target_pairs={{1,0},{2,1},{3,2},{4,3},{5,4},{6,5},{7,6},{0,7},{9,8},{10,9},{11,1... | collective-permute-start | bytes 3080 | tf_op jit(solution)/shard_map/ppermute | solution.py:34
  14.8 0.2 fusion.1
  15.1 1.3 fusion.27
  16.4 0.6 gather_fusion
  17.0 0.1 add_compare_fusion
  17.1 0.1 iota_compare_fusion
  17.2 2.4 collective-permute-done
  19.6 4.8 collective-permute-done.1
  24.4 3.3 collective-permute-start.5
  27.7 1.5 collective-permute-done.2
  29.2 0.3 copy.97
  29.4 0.3 copy.96
  29.7 3.3 collective-permute-start.6
  33.0 0.9 collective-permute-done.3
  34.0 0.3 collective-permute-done.6
  34.4 0.6 gather_fusion.1
  35.0 24.7 %all-gather = bf16[32,2,1536]{2,1,0:T(2,128)(2,1)S(1)} all-gather(bf16[1,2,1536]{2,1,0:T(2,128)(2,1)S(1)} %get-tuple-element.19), channel_id=1, replica_groups=mesh['group'=32,'tp'=8] {'group'}, dimensions={0}, use_global_device_ids=true | all-gather | bytes 202752 | tf_op jit(solution)/shard_map/all_gather | solution.py:39
  59.6 0.1 reshape.227
  59.7 0.6 gather_fusion.2
  60.3 0.3 select_reduce_fusion
  60.6 0.1 copy.81
  60.7 0.1 select_reduce_fusion.1
  60.8 0.1 copy.82
  61.0 0.1 fusion.29
  61.1 0.1 reshape.187
  61.2 0.2 convert_reduce_fusion
  61.4 0.1 copy.86
  61.5 76.4 %pmax.7 = f32[64,12]{1,0:T(8,128)S(1)} all-reduce(f32[64,12]{1,0:T(8,128)S(1)} %copy.86), channel_id=1, replica_groups=mesh['group'=32,'tp'=8] {'group','tp'}, use_global_device_ids=true, to_apply=%region_4.5 | all-reduce | flops 768 | bytes 6144 | tf_op jit(solution)/shard_map/pmax | solution.py:76
  137.9 0.6 gather_fusion.3
  138.5 0.2 fusion.5
  138.7 0.1 copy.88
  138.8 73.5 %psum.15 = f32[64,12]{1,0:T(8,128)S(1)} all-reduce(f32[64,12]{1,0:T(8,128)S(1)} %get-tuple-element.10), channel_id=1, replica_groups=mesh['group'=32,'tp'=8] {'group','tp'}, use_global_device_ids=true, to_apply=%region_7.8 | all-reduce | flops 768 | bytes 6144 | tf_op jit(solution)/shard_map/psum | solution.py:78
  212.4 0.1 broadcast_bitcast_fusion.2
  212.5 0.4 convolution_multiply_fusion
  212.9 0.4 fusion.2
  213.3 0.2 copy.84
  213.6 0.1 reshape.182
  213.7 0.2 broadcast_in_dim.105
  213.9 0.9 bitcast_multiply_fusion
  214.8 0.0 reduce-scatter.4.cloned.1.call-start
  214.9 0.1 broadcast_bitcast_fusion
  215.0 243.7 %all-reduce.2.cloned.1.call-done = f32[64,1536]{1,0:T(8,128)} async-done(((f32[64,1536]{1,0:T(8,128)}), f32[64,1536]{1,0:T(8,128)}) %all-reduce.2.cloned.1.call-update) | async-done | bytes 393232 | tf_op jit(solution)/shard_map/psum | solution.py:78
  458.6 2.7 convolution_bitcast_fusion
  461.3 0.0 reduce-scatter.4.cloned.1.call-update
  461.3 39.5 %reduce-scatter.4.cloned.1.call-done = f32[384,2]{1,0:T(8,128)} async-done(((f32[3072,2]{1,0:T(8,128)}), f32[384,2]{1,0:T(8,128)}) %reduce-scatter.4.cloned.1.call-update) | async-done | bytes 3088
  500.9 1.6 copy.95
  (45 shorter events, 0.3 us)
Async XLA Ops:
  6.5 1.4 copy-start
  6.5 8.3 %copy-start.3 = (s32[64,32]{0,1:T(8,128)S(1)}, s32[64,32]{0,1:T(8,128)}, u32[]{:S(2)}) copy-start(s32[64,32]{0,1:T(8,128)} %param.10) | copy-start | bytes 24580
  6.5 9.8 %copy-start.1 = (s32[64]{0:T(128)S(1)}, s32[64]{0:T(128)}, u32[]{:S(2)}) copy-start(s32[64]{0:T(128)} %param.11) | copy-start | bytes 772
  6.5 452.1 %all-reduce.2.cloned.1.call-start = ((), (), s32[]{:S(2)}) async-start(), calls=%async_computation.1 | async-start | bytes 786432 | tf_op jit(solution)/shard_map/psum | solution.py:78
  9.0 15.4 %collective-permute-start.4 = (bf16[2,256]{1,0:T(2,128)(2,1)S(1)}, bf16[2,256]{1,0:T(2,128)(2,1)S(1)}, u32[]{:S(2)}, u32[]{:S(2)}) collective-permute-start(bf16[2,256]{1,0:T(2,128)(2,1)S(1)} %convolution_convert_fusion), channel_id=1, source_target_pairs={{1,0},{2,1},{3,2},{4,3},{5,4},{6,5},{7,6},{0,7},{9,8},{10,9},{11,1... | collective-permute-start | bytes 3080 | tf_op jit(solution)/shard_map/ppermute | solution.py:34
  14.8 4.8 collective-permute-start
  19.6 4.8 collective-permute-start.1
  24.4 4.8 collective-permute-start.2
  24.4 5.3 %collective-permute-start.5 = (bf16[2,256]{1,0:T(2,128)(2,1)S(1)}, bf16[2,256]{1,0:T(2,128)(2,1)S(1)}, u32[]{:S(2)}, u32[]{:S(2)}) collective-permute-start(bf16[2,256]{1,0:T(2,128)(2,1)S(1)} %collective-permute-done.4), channel_id=1, source_target_pairs={{1,0},{2,1},{3,2},{4,3},{5,4},{6,5},{7,6},{0,7},{9,8},{10,9},{11,1... | collective-permute-start | bytes 3080 | tf_op jit(solution)/shard_map/ppermute | solution.py:34
  29.2 4.8 collective-permute-start.3
  29.7 4.6 collective-permute-start.6
  213.7 245.0 %copy-start.2 = (bf16[192,3072]{1,0:T(8,128)(2,1)S(1)}, bf16[192,3072]{1,0:T(8,128)(2,1)}, u32[]{:S(2)}) copy-start(bf16[192,3072]{1,0:T(8,128)(2,1)} %param.8) | copy-start | bytes 3538948
  214.8 286.1 %reduce-scatter.4.cloned.1.call-start = ((), (), s32[]{:S(2)}) async-start(), calls=%async_computation.2 | async-start | bytes 1769472
Sparse Core Ops, SparseCore 0:
  214.9 243.6 all-reduce.1
  461.5 39.3 reduce-scatter.3
